TPU v7x, 256 devices: a whole 4x4x8 slice. The times are simulated.
256 devices in a mesh: shell: 8 (over z), sector: 32 (over x, y, core).
Axes of the slice: x: 4, y: 4, z: 8, core: 2. Of those that a mesh axis runs over, the one named last changes fastest.
Arguments:
- bricks: bfloat16 [8, 256, 32, 512], P('shell', 'sector'), may hold values from -6 to 6
- conv_w: bfloat16 [32, 864], replicated, may hold values from -0.21875 to 0.21875
- conv_b: float32 [32], replicated, may hold values from -3 to 3
- head_w1: bfloat16 [32, 64], replicated, may hold values from -1 to 1
- head_b1: float32 [64], replicated, may hold values from -3 to 3
- head_w2: float32 [64, 2], replicated, may hold values from -0.75 to 0.75
- queries: int32 [8, 1024, 256], P('shell', 'sector'), may hold values from -1 to 4095, as said below
- sample_src: int32 [8, 131072], P('shell', 'sector'), may hold values from 0 to 8191, as said below
- depth_target: float32 [16384], P('sector'), may hold values from 0.1 to 0.9
- inten_target: float32 [16384], P('sector'), may hold values from 0 to 1
- drop_label: int32 [16384], P('sector'), may hold values 0 or 1
Outputs:
- loss_mean: float32 [], replicated
- grad_conv_w: float32 [32, 864], replicated
- grad_conv_b: float32 [32], replicated
- grad_head_w1: float32 [32, 64], replicated
- grad_head_b1: float32 [64], replicated
- grad_head_w2: float32 [64, 2], replicated
- grad_bricks: bfloat16 [8, 256, 32, 512], P('shell', 'sector')
- ray_depth: float32 [16384], P('sector')
Inputs may be any that keep to these rules, and one draw needn't show every extreme that they name: `queries`: entry of the buffer from a device of sector v to owner w: a cell address (brick of the owner times 512 plus cell) or -1 for an empty slot. Every sample of a device holds exactly one live slot, named by sample_src as w * 256 + slot. In every shell one owner receives full buffers of 256 from every sector. `sample_src`: A slot w * 256 + slot of the sample's own device; distinct samples of a device have distinct slots.
All inputs are finite; a program needn't handle non-finite values. No bound on the sum of `drop_label` on one device may be relied on, other than what follows from the above.
Results may differ from a plain program's by a relative error of at most 0.0015.
The roundings to bfloat16 on the way count: a program that leaves them out, or rounds other values in their place, can miss the bound.
Values may be sent and summed in bfloat16 or wider, within the bound.
No kernel may reach another device: no remote copies, remote signals or barrier semaphores. Data moves between devices by JAX's collectives and lax.ppermute only.
A program may use at most 192 MiB of HBM per device.

v0:
```python
import math
import jax
import jax.numpy as jnp
from jax import lax
from jax.sharding import PartitionSpec as P

SAMP = 8
HIGHEST = lax.Precision.HIGHEST
CUBE_OFFSETS = [(a, b, c) for a in range(3) for b in range(3) for c in range(3)]


def entering(value, axis, join, neutral, backward):
    count, mine = (lax.axis_size(axis), lax.axis_index(axis))
    pieces = lax.all_gather(value, axis)
    if backward:
        pieces = pieces[::-1]
        mine = count - 1 - mine
    total = jnp.full_like(value, 0) + jnp.asarray(neutral, value.dtype)

    def hop(position, total):
        longer = join(total, pieces[position])
        return jnp.where(position < mine, longer, total)

    return lax.fori_loop(0, count - 1, hop, total)


def unfold_cells(block_set):
    brick_count = block_set.shape[0]
    channel_width = block_set.shape[1]
    cube = block_set.reshape(brick_count, channel_width, 8, 8, 8)
    padded = jnp.pad(cube, ((0, 0), (0, 0), (1, 1), (1, 1), (1, 1)))
    columns = [
        padded[:, :, a : a + 8, b : b + 8, c : c + 8].reshape(brick_count, channel_width, 512)
        for a, b, c in CUBE_OFFSETS
    ]
    return jnp.stack(columns, axis=1).reshape(brick_count, 27 * channel_width, 512)


def conv_backward(block_set, block_cot, conv_w, conv_b):
    unfolded = unfold_cells(block_set)
    pre_act = (
        jnp.einsum("oc,bcn->obn", conv_w, unfolded, preferred_element_type=jnp.float32)
        + conv_b[:, None, None]
    )
    _, gelu_pull = jax.vjp(jax.nn.gelu, pre_act)
    pre_grad = gelu_pull(block_cot)[0].astype(jnp.bfloat16)
    weight_grad = jnp.einsum("obn,bcn->oc", pre_grad, unfolded, preferred_element_type=jnp.float32)
    bias_grad = jnp.sum(pre_grad.astype(jnp.float32), axis=(1, 2))
    column_grad = jnp.einsum("oc,obn->bcn", conv_w, pre_grad, preferred_element_type=jnp.float32)
    _, fold_pull = jax.vjp(unfold_cells, jnp.zeros(block_set.shape, jnp.float32))
    block_grad = fold_pull(column_grad)[0]
    return (weight_grad, bias_grad, block_grad.astype(jnp.bfloat16))


def field_head(feature_cols, weight_one, bias_one, weight_two):
    hidden = (
        jnp.einsum("ch,cm->hm", weight_one, feature_cols, precision=HIGHEST) + bias_one[:, None]
    )
    outputs = jnp.einsum("hk,hm->km", weight_two, jax.nn.gelu(hidden), precision=HIGHEST)
    return (jax.nn.softplus(outputs[0]), jax.nn.sigmoid(outputs[1]))


def render_terms(density, intensity, depth_grid, step_size):
    optical = density * step_size
    before = jnp.cumsum(optical, axis=-1) - optical
    weights = jnp.exp(-before) * (1.0 - jnp.exp(-optical))
    return (
        jnp.sum(weights * depth_grid, axis=-1),
        jnp.sum(weights * intensity, axis=-1),
        jnp.sum(optical, axis=-1),
    )


def add_terms(first_term, second_term):
    return first_term + second_term


def local(
    bricks,
    conv_w,
    conv_b,
    head_w1,
    head_b1,
    head_w2,
    queries,
    sample_src,
    depth_target,
    inten_target,
    drop_label,
):
    shells = lax.axis_size("shell")
    sectors = lax.axis_size("sector")
    shell_index = lax.axis_index("shell")
    local_bricks = bricks[0]
    brick_count = local_bricks.shape[0]
    channels = local_bricks.shape[1]
    group_size = math.gcd(brick_count, 8)
    group_cols = group_size * 512
    group_total = brick_count // group_size
    weight_one = head_w1.astype(jnp.float32)
    brick_groups = local_bricks.reshape(group_total, group_size, channels, 512)

    def decode_group(group_id, table_now):
        block_set = lax.dynamic_index_in_dim(brick_groups, group_id, 0, keepdims=False)
        pre_act = (
            jnp.einsum(
                "oc,bcn->obn", conv_w, unfold_cells(block_set), preferred_element_type=jnp.float32
            )
            + conv_b[:, None, None]
        )
        values = jax.nn.gelu(pre_act).astype(jnp.bfloat16).reshape(channels, group_cols)
        return values

    cell_table = lax.fori_loop(
        0, group_total, decode_group, jnp.zeros((channels, brick_count * 512), jnp.bfloat16)
    )
    requests = queries[0]
    capacity = requests.shape[1]
    owner_addr = lax.all_to_all(
        requests, "sector", split_axis=0, concat_axis=0, tiled=True
    ).reshape(-1)
    live_slot = owner_addr >= 0
    picked = jnp.take(cell_table, jnp.where(live_slot, owner_addr, 0), axis=1)
    owner_feats = jnp.where(live_slot[None, :], picked, jnp.zeros((), jnp.bfloat16))
    sources = sample_src[0]
    replies = lax.all_to_all(
        owner_feats.reshape(channels, sectors, capacity),
        "sector",
        split_axis=1,
        concat_axis=1,
        tiled=True,
    )
    sample_cols = jnp.take(replies.reshape(channels, sectors * capacity), sources, axis=1).astype(
        jnp.float32
    )
    (density, intensity), head_pull = jax.vjp(field_head, sample_cols, weight_one, head_b1, head_w2)
    ray_count = sources.shape[0] // SAMP
    density = density.reshape(ray_count, SAMP)
    intensity = intensity.reshape(ray_count, SAMP)
    step_size = 2.0 / (shells * SAMP)
    depth_grid = (
        shell_index.astype(jnp.float32) * SAMP + jnp.arange(SAMP, dtype=jnp.float32) + 0.5
    ) / (shells * SAMP)

    def local_render(dens_in, inten_in):
        return render_terms(dens_in, inten_in, depth_grid, step_size)

    (shell_depth, shell_inten, shell_tau), render_pull = jax.vjp(local_render, density, intensity)
    dropped = drop_label.astype(jnp.float32)
    kept_weight = 1.0 - dropped
    zeros_rays = jnp.zeros_like(shell_tau)
    prefix = entering(shell_tau, "shell", add_terms, zeros_rays, False)
    entry_trans = jnp.exp(-prefix)
    ray_depth, ray_inten, tau_total = lax.psum(
        (entry_trans * shell_depth, entry_trans * shell_inten, shell_tau), "shell"
    )
    escape = jnp.exp(-tau_total)
    grad_depth = 2.0 * kept_weight * (ray_depth - depth_target)
    grad_inten = 2.0 * kept_weight * (ray_inten - inten_target)
    own_weight = (grad_depth * shell_depth + grad_inten * shell_inten) * entry_trans
    behind = entering(own_weight, "shell", add_terms, zeros_rays, True)
    grad_escape = 2.0 * (escape - dropped)
    dens_grad, inten_grad = render_pull(
        (grad_depth * entry_trans, grad_inten * entry_trans, -grad_escape * escape - behind)
    )
    ray_loss = jnp.sum(
        kept_weight * ((ray_depth - depth_target) ** 2 + (ray_inten - inten_target) ** 2)
        + (escape - dropped) ** 2
    )
    loss_mean = lax.psum(ray_loss, "sector") / (ray_count * sectors)
    sample_grad, grad_one, grad_bias_one, grad_two = head_pull(
        (dens_grad.reshape(-1), inten_grad.reshape(-1))
    )
    buckets = jnp.zeros((channels, sectors * capacity), jnp.float32).at[:, sources].set(sample_grad)
    owner_grad = lax.all_to_all(
        buckets.reshape(channels, sectors, capacity),
        "sector",
        split_axis=1,
        concat_axis=1,
        tiled=True,
    ).reshape(channels, sectors * capacity)
    target_index = jnp.where(live_slot, owner_addr, brick_count * 512)
    table_grad = (
        jnp.zeros((channels, brick_count * 512), jnp.float32)
        .at[:, target_index]
        .add(owner_grad, mode="drop")
    )

    def conv_back(totals, group_id):
        block_set = lax.dynamic_index_in_dim(brick_groups, group_id, 0, keepdims=False)
        block_cot = table_grad.reshape(channels, group_size, 512)
        weight_grad, bias_grad, block_grad = conv_backward(block_set, block_cot, conv_w, conv_b)
        return ((totals[0] + weight_grad, totals[1] + bias_grad), block_grad)

    start = (jnp.zeros(conv_w.shape, jnp.float32), jnp.zeros_like(conv_b))
    (conv_grad, conv_bias_grad), brick_grads = lax.scan(
        conv_back, start, jnp.arange(group_total, dtype=jnp.int32)
    )
    summed = lax.psum(
        (conv_grad, conv_bias_grad, grad_one, grad_bias_one, grad_two), ("shell", "sector")
    )
    return (
        loss_mean,
        summed[0],
        summed[1],
        summed[2],
        summed[3],
        summed[4],
        brick_grads,
        ray_depth,
    )


def solution(mesh):
    return jax.shard_map(
        local,
        mesh=mesh,
        in_specs=(
            P("shell", "sector", None, None),
            P(),
            P(),
            P(),
            P(),
            P(),
            P("shell", "sector", None),
            P("shell", "sector"),
            P("sector"),
            P("sector"),
            P("sector"),
        ),
        out_specs=(P(), P(), P(), P(), P(), P(), P("shell", "sector", None, None), P("sector")),
        check_vma=False,
    )
```

profile of v0, /device:TPU:1, one launch (start us, length us, event | category | flops | bytes accessed | tf_op | source)
XLA Modules:
  0.0 665.0 jit_solution(13087959850178110753)
XLA Ops:
  8.6 8.6 %all-to-all-start = ((s32[32,1,256]{2,1,0:T(1,128)}), s32[32,1,256]{2,1,0:T(1,128)S(1)}, u32[]{:S(2)}, u32[]{:S(2)}) async-start(s32[32,1,256]{2,1,0:T(1,128)} %all_to_all.12), calls=%async_computation | async-start | bytes 65536 | tf_op jit(solution)/shard_map/all_to_all | solution.py:119
  18.6 3.4 pad_slice_fusion.1
  22.1 6.8 %pad_slice_fusion = (bf16[8,32,8,8,8]{1,4,3,2,0:T(8,128)(2,1)}, bf16[8,32,8,8,8]{1,4,3,2,0:T(8,128)(2,1)}, bf16[8,32,8,8,8]{1,4,3,2,0:T(8,128)(2,1)}, bf16[8,32,...) fusion(bf16[8,32,8,8,8]{1,4,3,2,0:T(8,128)(2,1)S(1)} %bitcast.139), kind=kLoop, calls=%fused_computation.8 | loop fusion | bytes 5242880 | tf_op jit(solution)/shard_map/while/body/eval_jaxpr/slice | solution.py:33
  118.1 5.1 multiply_convert_fusion
  124.4 24.0 %gather_fusion = bf16[8192,32]{1,0:T(8,128)(2,1)S(1)} fusion(bf16[32,4096]{0,1:T(8,128)(2,1)S(1)} %bitcast.136, s32[8192]{0:T(1024)S(1)} %broadcast_clamp_fusion), kind=kCustom, calls=%fused_computation | custom fusion | bytes 1081344 | tf_op jit(solution)/shard_map/jit(_take)/gather | solution.py:123
  150.3 7.4 %all-to-all-start.1 = ((bf16[32,32,256]{2,0,1:T(8,128)(2,1)}), bf16[32,32,256]{2,0,1:T(8,128)(2,1)S(1)}, u32[]{:S(2)}, u32[]{:S(2)}) async-start(bf16[32,32,256]{2,0,1:T(8,128)(2,1)} %select_select_fusion), calls=%async_computation.1 | async-start | bytes 1048576 | tf_op jit(solution)/shard_map/all_to_all | solution.py:126
  157.8 11.5 %all-to-all-done.1 = bf16[32,32,256]{2,0,1:T(8,128)(2,1)S(1)} async-done(((bf16[32,32,256]{2,0,1:T(8,128)(2,1)}), bf16[32,32,256]{2,0,1:T(8,128)(2,1)S(1)}, u32[]{:S(2)}, u32[]{:S(2)}) %all-to-all-start.1) | async-done | bytes 524320 | tf_op jit(solution)/shard_map/all_to_all | solution.py:126
  170.4 12.1 %gather_fusion.1 = bf16[4096,32]{1,0:T(8,128)(2,1)S(1)} fusion(bf16[32,8192]{0,1:T(8,128)(2,1)S(1)} %bitcast.163, s32[4096]{0:T(1024)S(1)} %broadcast_clamp_fusion.1), kind=kCustom, calls=%fused_computation.1 | custom fusion | bytes 540672 | tf_op jit(solution)/shard_map/jit(_take)/gather | solution.py:133
  187.0 19.6 %all-gather.2 = f32[8,1,512]{2,1,0:T(1,128)S(1)} all-gather(f32[1,1,512]{2,1,0:T(1,128)S(1)} %bitcast.209), channel_id=2, replica_groups=mesh['shell'=8,'sector'=32] {'shell'}, dimensions={0}, use_global_device_ids=true | all-gather | bytes 18432 | tf_op jit(solution)/shard_map/all_gather | solution.py:14
  207.0 11.4 %all-reduce.31 = (f32[512]{0:T(512)S(1)}, f32[512]{0:T(512)S(1)}, f32[512]{0:T(512)S(1)}) all-reduce(f32[512]{0:T(512)S(1)} %get-tuple-element.265, f32[512]{0:T(512)S(1)} %get-tuple-element.360, f32[512]{0:T(512)S(1)} %get-tuple-element.359), channel_id=1, replica_groups=mesh['shell'=8,'sector'=32] {'shell'}, use_global_device_ids=true, to_apply=%region_8.9 | all-reduce | flops 1536 | bytes 12288 | tf_op jit(solution)/shard_map/psum | solution.py:154
  220.8 15.9 %all-gather.3 = f32[8,1,512]{2,1,0:T(1,128)S(1)} all-gather(f32[1,1,512]{2,1,0:T(1,128)} %bitcast.210), channel_id=3, replica_groups=mesh['shell'=8,'sector'=32] {'shell'}, dimensions={0}, use_global_device_ids=true | all-gather | bytes 18432 | tf_op jit(solution)/shard_map/all_gather | solution.py:14
  239.9 2.4 fusion.56
  242.3 3.9 fusion.57
  246.2 13.2 %scatter_custom_fusion = f32[32,8192]{0,1:T(8,128)} fusion(s32[4096]{0:T(1024)S(1)} %bitcast.205, f32[4096,32]{1,0:T(8,128)} %fusion.57, f32[]{:T(128)} %constant.164.clone.1), kind=kCustom, calls=%fused_computation.45 | custom fusion | bytes 1049088 | tf_op jit(solution)/shard_map/scatter | solution.py:174
  259.5 3.6 copy.154
  263.1 18.7 %all-to-all-start.2 = ((f32[32,32,256]{2,0,1:T(8,128)}), f32[32,32,256]{2,0,1:T(8,128)S(1)}, u32[]{:S(2)}, u32[]{:S(2)}) async-start(f32[32,32,256]{2,0,1:T(8,128)} %copy.154), calls=%async_computation.2 | async-start | bytes 2097152 | tf_op jit(solution)/shard_map/all_to_all | solution.py:175
  281.8 71.8 %psum.66 = f32[]{:T(128)} all-reduce(f32[]{:T(128)} %get-tuple-element.354), channel_id=1, replica_groups=mesh['shell'=8,'sector'=32] {'sector'}, use_global_device_ids=true, to_apply=%region_10.11 | all-reduce | flops 1 | bytes 8 | tf_op jit(solution)/shard_map/psum | solution.py:170
  358.3 2.8 copy.156
  361.1 45.0 %scatter_custom_fusion.1 = f32[32,4096]{0,1:T(8,128)S(1)} fusion(s32[8192]{0:T(1024)} %bitcast.208, f32[8192,32]{1,0:T(8,128)} %copy.156, f32[]{:T(128)} %constant.164.clone.1), kind=kCustom, calls=%fused_computation.58 | custom fusion | flops 262144 | bytes 524800 | tf_op jit(solution)/shard_map/scatter-add | solution.py:186
  407.2 5.8 convolution_bitcast_fusion.2
  417.1 3.4 fusion.54
  422.1 3.0 copy.197
  425.1 3.0 copy.204
  428.1 3.0 copy.203
  431.0 3.0 copy.202
  434.0 3.0 copy.201
  437.0 3.0 copy.200
  440.0 3.0 copy.199
  443.0 3.0 copy.223
  445.9 3.0 copy.222
  448.9 3.0 copy.221
  451.9 3.0 copy.220
  454.9 3.0 copy.219
  457.9 3.0 copy.218
  460.9 3.0 copy.217
  463.9 3.0 copy.216
  466.9 3.0 copy.215
  469.8 3.0 copy.214
  472.8 3.0 copy.213
  475.9 3.0 copy.212
  478.8 3.0 copy.211
  481.8 3.0 copy.210
  484.8 3.0 copy.209
  487.8 3.0 copy.208
  490.8 3.2 copy.207
  497.9 16.8 %pad_add_fusion = f32[8,32,10,10,10]{1,4,3,2,0:T(8,128)S(1)} fusion(f32[8,32,8,8,8]{1,4,3,2,0:T(8,128)} %bitcast.148, f32[8,32,8,8,8]{1,4,3,2,0:T(8,128)} %bitcast.149, f32[8,32,8,8,8]{1,4,3,2,0:T(8,128)} %bitcast.150, f32[8,32,8,8,8]{1,4,3,2,0:T(8,128)} %bitcast.151, f32[8,32,8,8,8]{1,4,3,2,0:T(8,128)} %bitcast.152, f32[8,32,8,8,8]{1,4,3,2,0:T(8,128)} %bitcast.153, ...), kind=kLoop, calls=%fused_computation.34 | loop fusion | flops 5376000 | bytes 12558336 | tf_op jit(solution)/shard_map/while/body/eval_jaxpr/transpose(jvp())/add_any | solution.py:33
  515.8 72.8 %all-reduce.30 = (f32[32]{0:T(128)}, f32[32,64]{1,0:T(8,128)}, f32[64]{0:T(128)}, f32[64,2]{0,1:T(2,128)}) all-reduce(f32[32]{0:T(128)S(1)} %get-tuple-element.289, f32[32,64]{1,0:T(8,128)S(1)} %fusion.21, f32[64]{0:T(128)S(1)} %get-tuple-element.363, f32[64,2]{0,1:T(2,128)S(1)} %fusion.20), channel_id=1, replica_groups=mesh['shell'=8,'sector'=32] {'shell','sector'}, use_global_device_ids=true, to_apply=%region_18.19 | all-reduce | flops 2272 | bytes 18176 | tf_op jit(solution)/shard_map/psum | solution.py:199
  589.7 65.3 %all-reduce.34.cloned.1.call-done = f32[32,864]{1,0:T(8,128)} async-done(((f32[32,864]{1,0:T(8,128)}), f32[32,864]{1,0:T(8,128)}) %all-reduce.34.cloned.1.call-update) | async-done | bytes 110608 | tf_op jit(solution)/shard_map/psum | solution.py:199
  (200 shorter events, 125.2 us)
Async XLA Ops:
  7.2 110.9 %copy-start = (bf16[32,864]{1,0:T(8,128)(2,1)S(1)}, bf16[32,864]{1,0:T(8,128)(2,1)}, u32[]{:S(2)}) copy-start(bf16[32,864]{1,0:T(8,128)(2,1)} %param.16) | copy-start | bytes 165892
  8.6 115.1 %all-to-all-start = ((s32[32,1,256]{2,1,0:T(1,128)}), s32[32,1,256]{2,1,0:T(1,128)S(1)}, u32[]{:S(2)}, u32[]{:S(2)}) async-start(s32[32,1,256]{2,1,0:T(1,128)} %all_to_all.12), calls=%async_computation | async-start | bytes 65536 | tf_op jit(solution)/shard_map/all_to_all | solution.py:119
  22.1 6.8 %copy-start.18 = (s32[1,4096]{1,0:T(1,128)S(1)}, s32[1,4096]{1,0:T(1,128)}, u32[]{:S(2)}) copy-start(s32[1,4096]{1,0:T(1,128)} %param.22) | copy-start | bytes 49156
  28.9 13.6 %copy-start.9 = (bf16[8,32,8,8,8]{1,4,3,2,0:T(8,128)(2,1)S(1)}, bf16[8,32,8,8,8]{1,4,3,2,0:T(8,128)(2,1)}, u32[]{:S(2)}) copy-start(bf16[8,32,8,8,8]{1,4,3,2,0:T(8,128)(2,1)} %get-tuple-element.345) | copy-start | bytes 786436
  43.6 22.6 %copy-start.8 = (bf16[8,32,8,8,8]{1,4,3,2,0:T(8,128)(2,1)S(1)}, bf16[8,32,8,8,8]{1,4,3,2,0:T(8,128)(2,1)}, u32[]{:S(2)}) copy-start(bf16[8,32,8,8,8]{1,4,3,2,0:T(8,128)(2,1)} %get-tuple-element.330) | copy-start | bytes 786436
  61.7 30.3 %copy-start.12 = (bf16[1,8,32,512]{3,2,1,0:T(8,128)(2,1)S(1)}, bf16[1,8,32,512]{3,2,1,0:T(8,128)(2,1)}, u32[]{:S(2)}) copy-start(bf16[1,8,32,512]{3,2,1,0:T(8,128)(2,1)} %param.15) | copy-start | bytes 786436
  67.2 32.2 %copy-start.7 = (bf16[8,32,8,8,8]{1,4,3,2,0:T(8,128)(2,1)S(1)}, bf16[8,32,8,8,8]{1,4,3,2,0:T(8,128)(2,1)}, u32[]{:S(2)}) copy-start(bf16[8,32,8,8,8]{1,4,3,2,0:T(8,128)(2,1)} %get-tuple-element.336) | copy-start | bytes 786436
  92.7 23.9 %copy-start.13 = (bf16[8,1,32,512]{3,2,1,0:T(8,128)(2,1)S(1)}, bf16[8,1,32,512]{3,2,1,0:T(8,128)(2,1)}, u32[]{:S(2)}) copy-start(bf16[8,1,32,512]{3,2,1,0:T(8,128)(2,1)} %copy.147) | copy-start | bytes 786436
  95.0 23.1 %copy-start.27 = (f32[32]{0:T(128)S(1)}, f32[32]{0:T(128)}, u32[]{:S(2)}) copy-start(f32[32]{0:T(128)} %param.17) | copy-start | bytes 388
  100.5 13.9 %copy-start.17 = (bf16[8,1,32,512]{3,2,1,0:T(8,128)(2,1)S(1)}, bf16[8,1,32,512]{3,2,1,0:T(8,128)(2,1)}, u32[]{:S(2)}) copy-start(bf16[8,1,32,512]{3,2,1,0:T(8,128)(2,1)} %copy.144) | copy-start | bytes 786436
  100.5 14.6 %copy-start.15 = (bf16[8,1,32,512]{3,2,1,0:T(8,128)(2,1)S(1)}, bf16[8,1,32,512]{3,2,1,0:T(8,128)(2,1)}, u32[]{:S(2)}) copy-start(bf16[8,1,32,512]{3,2,1,0:T(8,128)(2,1)} %copy.145) | copy-start | bytes 786436
  100.5 15.3 %copy-start.14 = (bf16[8,1,32,512]{3,2,1,0:T(8,128)(2,1)S(1)}, bf16[8,1,32,512]{3,2,1,0:T(8,128)(2,1)}, u32[]{:S(2)}) copy-start(bf16[8,1,32,512]{3,2,1,0:T(8,128)(2,1)} %copy.146) | copy-start | bytes 786436
  100.5 16.8 %copy-start.16 = (bf16[8,1,32,512]{3,2,1,0:T(8,128)(2,1)S(1)}, bf16[8,1,32,512]{3,2,1,0:T(8,128)(2,1)}, u32[]{:S(2)}) copy-start(bf16[8,1,32,512]{3,2,1,0:T(8,128)(2,1)} %copy.148) | copy-start | bytes 786436
  124.4 58.2 %copy-start.19 = (bf16[32,64]{1,0:T(8,128)(2,1)S(1)}, bf16[32,64]{1,0:T(8,128)(2,1)}, u32[]{:S(2)}) copy-start(bf16[32,64]{1,0:T(8,128)(2,1)} %param.18) | copy-start | bytes 12292
  124.4 58.2 %copy-start.28 = (f32[64]{0:T(128)S(1)}, f32[64]{0:T(128)}, u32[]{:S(2)}) copy-start(f32[64]{0:T(128)} %param.19) | copy-start | bytes 772
  148.4 35.0 %copy-start.29 = (f32[64,2]{0,1:T(2,128)S(1)}, f32[64,2]{0,1:T(2,128)}, u32[]{:S(2)}) copy-start(f32[64,2]{0,1:T(2,128)} %param.20) | copy-start | bytes 1540
  150.3 19.0 %all-to-all-start.1 = ((bf16[32,32,256]{2,0,1:T(8,128)(2,1)}), bf16[32,32,256]{2,0,1:T(8,128)(2,1)S(1)}, u32[]{:S(2)}, u32[]{:S(2)}) async-start(bf16[32,32,256]{2,0,1:T(8,128)(2,1)} %select_select_fusion), calls=%async_computation.1 | async-start | bytes 1048576 | tf_op jit(solution)/shard_map/all_to_all | solution.py:126
  157.7 48.9 %copy-start.26 = (f32[8]{0:T(128)}, f32[8]{0:T(128)S(1)}, u32[]{:S(2)}) copy-start(f32[8]{0:T(128)S(1)} %add_multiply_fusion.1) | copy-start | bytes 100
  157.8 60.7 %copy-start.21 = (s32[512]{0:T(512)S(1)}, s32[512]{0:T(512)}, u32[]{:S(2)}) copy-start(s32[512]{0:T(512)} %param.25) | copy-start | bytes 6148
  157.8 60.7 %copy-start.23 = (f32[512]{0:T(512)S(1)}, f32[512]{0:T(512)}, u32[]{:S(2)}) copy-start(f32[512]{0:T(512)} %param.24) | copy-start | bytes 6148
  157.8 60.7 %copy-start.24 = (f32[512]{0:T(512)S(1)}, f32[512]{0:T(512)}, u32[]{:S(2)}) copy-start(f32[512]{0:T(512)} %param.23) | copy-start | bytes 6148
  183.4 58.9 %copy-start.11 = (f32[64,4096]{1,0:T(8,128)}, f32[64,4096]{1,0:T(8,128)S(1)}, u32[]{:S(2)}) copy-start(f32[64,4096]{1,0:T(8,128)S(1)} %fusion) | copy-start | bytes 3145732
  218.4 1.2 copy-start.22
  218.5 1.2 copy-start.25
  219.7 0.9 copy-start.20
  263.1 95.2 %all-to-all-start.2 = ((f32[32,32,256]{2,0,1:T(8,128)}), f32[32,32,256]{2,0,1:T(8,128)S(1)}, u32[]{:S(2)}, u32[]{:S(2)}) async-start(f32[32,32,256]{2,0,1:T(8,128)} %copy.154), calls=%async_computation.2 | async-start | bytes 2097152 | tf_op jit(solution)/shard_map/all_to_all | solution.py:175
  281.7 373.3 %all-reduce.34.cloned.1.call-start = ((), (), s32[]{:S(2)}) async-start(), calls=%async_computation.3 | async-start | bytes 229376 | tf_op jit(solution)/shard_map/psum | solution.py:199
  358.2 48.5 %copy-start.10 = (f32[32,8,512]{2,0,1:T(8,128)S(1)}, f32[32,8,512]{2,0,1:T(8,128)}, u32[]{:S(2)}) copy-start(f32[32,8,512]{2,0,1:T(8,128)} %get-tuple-element.362) | copy-start | bytes 1572868
  497.9 16.8 %copy-start.2 = (f32[8,1,32,512]{2,3,0,1:T(8,128)S(1)}, f32[8,1,32,512]{2,3,0,1:T(8,128)}, u32[]{:S(2)}) copy-start(f32[8,1,32,512]{2,3,0,1:T(8,128)} %copy.223) | copy-start | bytes 1572868
  497.9 16.8 %copy-start.3 = (f32[8,1,32,512]{2,3,0,1:T(8,128)S(1)}, f32[8,1,32,512]{2,3,0,1:T(8,128)}, u32[]{:S(2)}) copy-start(f32[8,1,32,512]{2,3,0,1:T(8,128)} %copy.222) | copy-start | bytes 1572868
  497.9 16.8 %copy-start.4 = (f32[8,1,32,512]{2,3,0,1:T(8,128)S(1)}, f32[8,1,32,512]{2,3,0,1:T(8,128)}, u32[]{:S(2)}) copy-start(f32[8,1,32,512]{2,3,0,1:T(8,128)} %copy.221) | copy-start | bytes 1572868
  497.9 16.8 %copy-start.5 = (f32[8,1,32,512]{2,3,0,1:T(8,128)S(1)}, f32[8,1,32,512]{2,3,0,1:T(8,128)}, u32[]{:S(2)}) copy-start(f32[8,1,32,512]{2,3,0,1:T(8,128)} %copy.220) | copy-start | bytes 1572868
  497.9 16.8 %copy-start.6 = (f32[8,1,32,512]{2,3,0,1:T(8,128)S(1)}, f32[8,1,32,512]{2,3,0,1:T(8,128)}, u32[]{:S(2)}) copy-start(f32[8,1,32,512]{2,3,0,1:T(8,128)} %copy.219) | copy-start | bytes 1572868
  514.7 141.9 %copy-start.1 = (bf16[32,864]{1,0:T(8,128)(2,1)S(1)}, bf16[32,864]{1,0:T(8,128)(2,1)}, u32[]{:S(2)}) copy-start(bf16[32,864]{1,0:T(8,128)(2,1)} %param.16) | copy-start | bytes 165892
Sparse Core Ops, SparseCore 0:
  420.6 234.3 all-reduce.33
where the time goes:
time: 677 us; the launch traced here: 665 us
  local copies, waits for them, and re-layouts  249 us (37%)
  blocking collectives  192 us (28%)
  waiting for transfers between devices  76.9 us (11%)
  other arithmetic  70.1 us (10%)
  starting transfers between devices  34.7 us (5%)
  matrix products  25.1 us (4%)
  between operations  16.9 us (2%)
    unnamed x118, local copies, waits for them, and re-layouts  119 us
    psum x1, blocking collectives, local(): lax.psum((conv_grad, conv_bias_grad, grad_one, grad_bias_one, grad_two),...  72.8 us
    psum x1, blocking collectives, local(): loss_mean = lax.psum(ray_loss, 'sector') / (ray_count * sectors)  71.8 us
    psum x1, waiting for transfers between devices, local(): lax.psum((conv_grad, conv_bias_grad, grad_one, grad_bias_one, grad_two),...  65.3 us
    reshape x26, local copies, waits for them, and re-layouts, unfold_cells(): jnp.stack(columns, axis=1).reshape(brick_count, 27 * channel_width, 512)  51.4 us
    scatter-add x1, other arithmetic, local(): table_grad = jnp.zeros((channels, brick_count * 512), jnp.float32).at[:,...  45 us
    all_gather x2, blocking collectives, entering(): pieces = lax.all_gather(value, axis)  35.5 us
    gather x2, local copies, waits for them, and re-layouts, local(): picked = jnp.take(cell_table, jnp.where(live_slot, owner_addr, 0), axis=1)  25 us
  transfers between devices with their start and end apart: 4, of which 2 were waited for; matrix products, arithmetic and copies ran while one was open for 31% of the time, Pallas kernels for 0%

commit v1 on v0

--- a/solution.py
+++ b/solution.py
@@ -197,7 +197,7 @@
         conv_back, start, jnp.arange(group_total, dtype=jnp.int32)
     )
     summed = lax.psum(
-        (conv_grad, conv_bias_grad, grad_one, grad_bias_one, grad_two), ("shell", "sector")
+        lax.psum((conv_grad, conv_bias_grad, grad_one, grad_bias_one, grad_two), "sector"), "shell"
     )
     return (
         loss_mean,

time: 677 us -> 650 us (0.960)
  the two profiles are of different devices: /device:TPU:1 before, /device:TPU:0 now
where the time goes in v1:
time: 650 us; the launch traced here: 638 us
  local copies, waits for them, and re-layouts  248 us (38%)
  blocking collectives  221 us (34%)
  other arithmetic  75.5 us (12%)
  waiting for transfers between devices  34.1 us (5%)
  matrix products  25.1 us (4%)
  starting transfers between devices  17.6 us (3%)
  between operations  16.8 us (3%)
    psum x1, blocking collectives, local(): loss_mean = lax.psum(ray_loss, 'sector') / (ray_count * sectors)  128 us
    unnamed x108, local copies, waits for them, and re-layouts  117 us
    reshape x26, local copies, waits for them, and re-layouts, unfold_cells(): jnp.stack(columns, axis=1).reshape(brick_count, 27 * channel_width, 512)  51.4 us
    all_gather x2, blocking collectives, entering(): pieces = lax.all_gather(value, axis)  46.4 us
    scatter-add x1, other arithmetic, local(): table_grad = jnp.zeros((channels, brick_count * 512), jnp.float32).at[:,...  44.8 us
    psum x1, blocking collectives, local(): lax.psum(lax.psum((conv_grad, conv_bias_grad, grad_one, grad_bias_one, gr...  30.8 us
    gather x2, local copies, waits for them, and re-layouts, local(): picked = jnp.take(cell_table, jnp.where(live_slot, owner_addr, 0), axis=1)  25 us
    add_any x1, other arithmetic, unfold_cells(): padded[:, :, a:a + 8, b:b + 8, c:c + 8]  18.2 us
  transfers between devices with their start and end apart: 5, of which 3 were waited for; matrix products, arithmetic and copies ran while one was open for 33% of the time, Pallas kernels for 0%

profile of v1, /device:TPU:0, one launch (start us, length us, event | category | flops | bytes accessed | tf_op | source)
XLA Modules:
  0.0 638.1 jit_solution(3421869750454156180)
XLA Ops:
  8.6 5.6 all-to-all-start
  15.6 3.4 pad_slice_fusion.1
  19.0 6.8 %pad_slice_fusion = (bf16[8,32,8,8,8]{1,4,3,2,0:T(8,128)(2,1)}, bf16[8,32,8,8,8]{1,4,3,2,0:T(8,128)(2,1)}, bf16[8,32,8,8,8]{1,4,3,2,0:T(8,128)(2,1)}, bf16[8,32,...) fusion(bf16[8,32,8,8,8]{1,4,3,2,0:T(8,128)(2,1)S(1)} %bitcast.139), kind=kLoop, calls=%fused_computation.8 | loop fusion | bytes 5242880 | tf_op jit(solution)/shard_map/while/body/eval_jaxpr/slice | solution.py:33
  115.1 5.1 multiply_convert_fusion
  121.4 24.0 %gather_fusion = bf16[8192,32]{1,0:T(8,128)(2,1)S(1)} fusion(bf16[32,4096]{0,1:T(8,128)(2,1)S(1)} %bitcast.136, s32[8192]{0:T(1024)S(1)} %broadcast_clamp_fusion), kind=kCustom, calls=%fused_computation | custom fusion | bytes 1081344 | tf_op jit(solution)/shard_map/jit(_take)/gather | solution.py:123
  147.4 7.4 %all-to-all-start.1 = ((bf16[32,32,256]{2,0,1:T(8,128)(2,1)}), bf16[32,32,256]{2,0,1:T(8,128)(2,1)S(1)}, u32[]{:S(2)}, u32[]{:S(2)}) async-start(bf16[32,32,256]{2,0,1:T(8,128)(2,1)} %select_select_fusion), calls=%async_computation.1 | async-start | bytes 1048576 | tf_op jit(solution)/shard_map/all_to_all | solution.py:126
  154.9 11.1 %all-to-all-done.1 = bf16[32,32,256]{2,0,1:T(8,128)(2,1)S(1)} async-done(((bf16[32,32,256]{2,0,1:T(8,128)(2,1)}), bf16[32,32,256]{2,0,1:T(8,128)(2,1)S(1)}, u32[]{:S(2)}, u32[]{:S(2)}) %all-to-all-start.1) | async-done | bytes 524320 | tf_op jit(solution)/shard_map/all_to_all | solution.py:126
  167.0 12.1 %gather_fusion.1 = bf16[4096,32]{1,0:T(8,128)(2,1)S(1)} fusion(bf16[32,8192]{0,1:T(8,128)(2,1)S(1)} %bitcast.163, s32[4096]{0:T(1024)S(1)} %broadcast_clamp_fusion.1), kind=kCustom, calls=%fused_computation.1 | custom fusion | bytes 540672 | tf_op jit(solution)/shard_map/jit(_take)/gather | solution.py:133
  183.6 25.4 %all-gather.2 = f32[8,1,512]{2,1,0:T(1,128)S(1)} all-gather(f32[1,1,512]{2,1,0:T(1,128)S(1)} %bitcast.209), channel_id=2, replica_groups=mesh['shell'=8,'sector'=32] {'shell'}, dimensions={0}, use_global_device_ids=true | all-gather | bytes 18432 | tf_op jit(solution)/shard_map/all_gather | solution.py:14
  209.4 15.7 %all-reduce.32 = (f32[512]{0:T(512)S(1)}, f32[512]{0:T(512)S(1)}, f32[512]{0:T(512)S(1)}) all-reduce(f32[512]{0:T(512)S(1)} %get-tuple-element.265, f32[512]{0:T(512)S(1)} %get-tuple-element.365, f32[512]{0:T(512)S(1)} %get-tuple-element.364), channel_id=1, replica_groups=mesh['shell'=8,'sector'=32] {'shell'}, use_global_device_ids=true, to_apply=%region_8.9 | all-reduce | flops 1536 | bytes 12288 | tf_op jit(solution)/shard_map/psum | solution.py:154
  227.4 21.0 %all-gather.3 = f32[8,1,512]{2,1,0:T(1,128)S(1)} all-gather(f32[1,1,512]{2,1,0:T(1,128)} %bitcast.210), channel_id=3, replica_groups=mesh['shell'=8,'sector'=32] {'shell'}, dimensions={0}, use_global_device_ids=true | all-gather | bytes 18432 | tf_op jit(solution)/shard_map/all_gather | solution.py:14
  254.0 4.0 fusion.57
  257.9 13.2 %scatter_custom_fusion = f32[32,8192]{0,1:T(8,128)} fusion(s32[4096]{0:T(1024)S(1)} %bitcast.205, f32[4096,32]{1,0:T(8,128)} %fusion.57, f32[]{:T(128)} %constant.164.clone.1), kind=kCustom, calls=%fused_computation.45 | custom fusion | bytes 1049088 | tf_op jit(solution)/shard_map/scatter | solution.py:174
  271.1 3.6 copy.154
  274.7 4.3 all-to-all-start.2
  283.0 12.8 %all-to-all-done.2 = f32[32,32,256]{2,0,1:T(8,128)S(1)} async-done(((f32[32,32,256]{2,0,1:T(8,128)}), f32[32,32,256]{2,0,1:T(8,128)S(1)}, u32[]{:S(2)}, u32[]{:S(2)}) %all-to-all-start.2) | async-done | bytes 1048608 | tf_op jit(solution)/shard_map/all_to_all | solution.py:175
  298.7 44.8 %scatter_custom_fusion.1 = f32[32,4096]{0,1:T(8,128)S(1)} fusion(s32[8192]{0:T(1024)} %bitcast.208, f32[8192,32]{1,0:T(8,128)} %copy.156, f32[]{:T(128)} %constant.164.clone.1), kind=kCustom, calls=%fused_computation.58 | custom fusion | flops 262144 | bytes 524800 | tf_op jit(solution)/shard_map/scatter-add | solution.py:186
  344.5 5.8 convolution_bitcast_fusion.2
  354.2 3.6 fusion.54
  359.8 3.0 copy.197
  362.8 3.0 copy.204
  365.8 3.0 copy.203
  368.8 3.0 copy.202
  371.8 3.0 copy.201
  374.8 3.0 copy.200
  377.8 3.0 copy.199
  380.7 3.0 copy.218
  383.7 3.0 copy.217
  386.7 3.0 copy.216
  389.8 3.0 copy.215
  392.8 3.0 copy.214
  395.7 3.0 copy.213
  398.7 2.9 copy.212
  401.6 3.0 copy.211
  404.7 3.0 copy.210
  407.7 3.0 copy.209
  410.7 3.0 copy.208
  413.7 3.0 copy.207
  416.6 3.0 copy.206
  419.6 3.0 copy.205
  422.6 18.2 %pad_add_fusion = f32[8,32,10,10,10]{1,4,3,2,0:T(8,128)} fusion(f32[8,32,8,8,8]{1,4,3,2,0:T(8,128)} %bitcast.148, f32[8,32,8,8,8]{1,4,3,2,0:T(8,128)} %bitcast.149, f32[8,32,8,8,8]{1,4,3,2,0:T(8,128)} %bitcast.150, f32[8,32,8,8,8]{1,4,3,2,0:T(8,128)} %bitcast.151, f32[8,32,8,8,8]{1,4,3,2,0:T(8,128)} %bitcast.152, f32[8,32,8,8,8]{1,4,3,2,0:T(8,128)} %bitcast.153, ...), kind=kLoop, calls=%fused_computation.34 | loop fusion | flops 5376000 | bytes 12558336 | tf_op jit(solution)/shard_map/while/body/eval_jaxpr/transpose(jvp())/add_any | solution.py:33
  441.4 3.0 copy.222
  444.4 3.0 copy.221
  447.5 3.0 copy.220
  452.4 10.2 %all-reduce.36.cloned.1.call-done = f32[32,864]{1,0:T(8,128)} async-done(((f32[32,864]{1,0:T(8,128)}), f32[32,864]{1,0:T(8,128)}) %all-reduce.36.cloned.1.call-update) | async-done | bytes 110608 | tf_op jit(solution)/shard_map/psum | solution.py:200
  462.6 5.3 fusion.1
  467.9 127.7 %all-reduce.30 = (f32[]{:T(128)}, f32[32]{0:T(128)S(1)}, f32[32,64]{1,0:T(8,128)S(1)}, f32[64]{0:T(128)S(1)}, f32[64,2]{0,1:T(2,128)S(1)}) all-reduce(f32[]{:T(128)} %get-tuple-element.359, f32[32]{0:T(128)S(1)} %get-tuple-element.294, f32[32,64]{1,0:T(8,128)S(1)} %fusion.21, ...), channel_id=1, replica_groups=mesh['shell'=8,'sector'=32] {'sector'}, use_global_device_ids=true, to_apply=%region_10.11 | all-reduce | flops 2273 | bytes 18184 | tf_op jit(solution)/shard_map/psum | solution.py:170
  597.4 30.8 %all-reduce.31 = (f32[32]{0:T(128)}, f32[32,64]{1,0:T(8,128)}, f32[64]{0:T(128)}, f32[64,2]{0,1:T(2,128)}) all-reduce(f32[32]{0:T(128)S(1)} %get-tuple-element.283, f32[32,64]{1,0:T(8,128)S(1)} %get-tuple-element.284, f32[64]{0:T(128)S(1)} %get-tuple-element.285, ...), channel_id=1, replica_groups=mesh['shell'=8,'sector'=32] {'shell'}, use_global_device_ids=true, to_apply=%region_20.21 | all-reduce | flops 2272 | bytes 18176 | tf_op jit(solution)/shard_map/psum | solution.py:199
  (193 shorter events, 128.0 us)
Async XLA Ops:
  7.2 107.9 %copy-start = (bf16[32,864]{1,0:T(8,128)(2,1)S(1)}, bf16[32,864]{1,0:T(8,128)(2,1)}, u32[]{:S(2)}) copy-start(bf16[32,864]{1,0:T(8,128)(2,1)} %param.16) | copy-start | bytes 165892
  8.6 112.1 %all-to-all-start = ((s32[32,1,256]{2,1,0:T(1,128)}), s32[32,1,256]{2,1,0:T(1,128)S(1)}, u32[]{:S(2)}, u32[]{:S(2)}) async-start(s32[32,1,256]{2,1,0:T(1,128)} %all_to_all.12), calls=%async_computation | async-start | bytes 65536 | tf_op jit(solution)/shard_map/all_to_all | solution.py:119
  19.0 6.9 %copy-start.13 = (s32[1,4096]{1,0:T(1,128)S(1)}, s32[1,4096]{1,0:T(1,128)}, u32[]{:S(2)}) copy-start(s32[1,4096]{1,0:T(1,128)} %param.22) | copy-start | bytes 49156
  25.9 13.6 %copy-start.4 = (bf16[8,32,8,8,8]{1,4,3,2,0:T(8,128)(2,1)S(1)}, bf16[8,32,8,8,8]{1,4,3,2,0:T(8,128)(2,1)}, u32[]{:S(2)}) copy-start(bf16[8,32,8,8,8]{1,4,3,2,0:T(8,128)(2,1)} %get-tuple-element.350) | copy-start | bytes 786436
  40.6 22.6 %copy-start.3 = (bf16[8,32,8,8,8]{1,4,3,2,0:T(8,128)(2,1)S(1)}, bf16[8,32,8,8,8]{1,4,3,2,0:T(8,128)(2,1)}, u32[]{:S(2)}) copy-start(bf16[8,32,8,8,8]{1,4,3,2,0:T(8,128)(2,1)} %get-tuple-element.335) | copy-start | bytes 786436
  58.6 30.3 %copy-start.7 = (bf16[1,8,32,512]{3,2,1,0:T(8,128)(2,1)S(1)}, bf16[1,8,32,512]{3,2,1,0:T(8,128)(2,1)}, u32[]{:S(2)}) copy-start(bf16[1,8,32,512]{3,2,1,0:T(8,128)(2,1)} %param.15) | copy-start | bytes 786436
  64.2 32.3 %copy-start.2 = (bf16[8,32,8,8,8]{1,4,3,2,0:T(8,128)(2,1)S(1)}, bf16[8,32,8,8,8]{1,4,3,2,0:T(8,128)(2,1)}, u32[]{:S(2)}) copy-start(bf16[8,32,8,8,8]{1,4,3,2,0:T(8,128)(2,1)} %get-tuple-element.341) | copy-start | bytes 786436
  89.7 23.9 %copy-start.8 = (bf16[8,1,32,512]{3,2,1,0:T(8,128)(2,1)S(1)}, bf16[8,1,32,512]{3,2,1,0:T(8,128)(2,1)}, u32[]{:S(2)}) copy-start(bf16[8,1,32,512]{3,2,1,0:T(8,128)(2,1)} %copy.147) | copy-start | bytes 786436
  92.0 23.1 %copy-start.22 = (f32[32]{0:T(128)S(1)}, f32[32]{0:T(128)}, u32[]{:S(2)}) copy-start(f32[32]{0:T(128)} %param.17) | copy-start | bytes 388
  97.6 13.8 %copy-start.12 = (bf16[8,1,32,512]{3,2,1,0:T(8,128)(2,1)S(1)}, bf16[8,1,32,512]{3,2,1,0:T(8,128)(2,1)}, u32[]{:S(2)}) copy-start(bf16[8,1,32,512]{3,2,1,0:T(8,128)(2,1)} %copy.144) | copy-start | bytes 786436
  97.6 14.6 %copy-start.10 = (bf16[8,1,32,512]{3,2,1,0:T(8,128)(2,1)S(1)}, bf16[8,1,32,512]{3,2,1,0:T(8,128)(2,1)}, u32[]{:S(2)}) copy-start(bf16[8,1,32,512]{3,2,1,0:T(8,128)(2,1)} %copy.145) | copy-start | bytes 786436
  97.6 15.3 %copy-start.9 = (bf16[8,1,32,512]{3,2,1,0:T(8,128)(2,1)S(1)}, bf16[8,1,32,512]{3,2,1,0:T(8,128)(2,1)}, u32[]{:S(2)}) copy-start(bf16[8,1,32,512]{3,2,1,0:T(8,128)(2,1)} %copy.146) | copy-start | bytes 786436
  97.6 16.8 %copy-start.11 = (bf16[8,1,32,512]{3,2,1,0:T(8,128)(2,1)S(1)}, bf16[8,1,32,512]{3,2,1,0:T(8,128)(2,1)}, u32[]{:S(2)}) copy-start(bf16[8,1,32,512]{3,2,1,0:T(8,128)(2,1)} %copy.148) | copy-start | bytes 786436
  121.4 57.7 %copy-start.14 = (bf16[32,64]{1,0:T(8,128)(2,1)S(1)}, bf16[32,64]{1,0:T(8,128)(2,1)}, u32[]{:S(2)}) copy-start(bf16[32,64]{1,0:T(8,128)(2,1)} %param.18) | copy-start | bytes 12292
  121.4 57.7 %copy-start.23 = (f32[64]{0:T(128)S(1)}, f32[64]{0:T(128)}, u32[]{:S(2)}) copy-start(f32[64]{0:T(128)} %param.19) | copy-start | bytes 772
  145.5 34.5 %copy-start.24 = (f32[64,2]{0,1:T(2,128)S(1)}, f32[64,2]{0,1:T(2,128)}, u32[]{:S(2)}) copy-start(f32[64,2]{0,1:T(2,128)} %param.20) | copy-start | bytes 1540
  147.4 18.6 %all-to-all-start.1 = ((bf16[32,32,256]{2,0,1:T(8,128)(2,1)}), bf16[32,32,256]{2,0,1:T(8,128)(2,1)S(1)}, u32[]{:S(2)}, u32[]{:S(2)}) async-start(bf16[32,32,256]{2,0,1:T(8,128)(2,1)} %select_select_fusion), calls=%async_computation.1 | async-start | bytes 1048576 | tf_op jit(solution)/shard_map/all_to_all | solution.py:126
  154.8 54.2 %copy-start.21 = (f32[8]{0:T(128)}, f32[8]{0:T(128)S(1)}, u32[]{:S(2)}) copy-start(f32[8]{0:T(128)S(1)} %add_multiply_fusion.1) | copy-start | bytes 100
  154.8 70.2 %copy-start.16 = (s32[512]{0:T(512)S(1)}, s32[512]{0:T(512)}, u32[]{:S(2)}) copy-start(s32[512]{0:T(512)} %param.25) | copy-start | bytes 6148
  154.8 70.2 %copy-start.18 = (f32[512]{0:T(512)S(1)}, f32[512]{0:T(512)}, u32[]{:S(2)}) copy-start(f32[512]{0:T(512)} %param.24) | copy-start | bytes 6148
  154.8 70.2 %copy-start.19 = (f32[512]{0:T(512)S(1)}, f32[512]{0:T(512)}, u32[]{:S(2)}) copy-start(f32[512]{0:T(512)} %param.23) | copy-start | bytes 6148
  180.0 74.0 %copy-start.6 = (f32[64,4096]{1,0:T(8,128)}, f32[64,4096]{1,0:T(8,128)S(1)}, u32[]{:S(2)}) copy-start(f32[64,4096]{1,0:T(8,128)S(1)} %fusion) | copy-start | bytes 3145732
  225.0 1.2 copy-start.17
  225.1 1.2 copy-start.20
  226.3 0.9 copy-start.15
  274.7 21.1 %all-to-all-start.2 = ((f32[32,32,256]{2,0,1:T(8,128)}), f32[32,32,256]{2,0,1:T(8,128)S(1)}, u32[]{:S(2)}, u32[]{:S(2)}) async-start(f32[32,32,256]{2,0,1:T(8,128)} %copy.154), calls=%async_computation.2 | async-start | bytes 2097152 | tf_op jit(solution)/shard_map/all_to_all | solution.py:175
  279.0 183.6 %all-reduce.36.cloned.1.call-start = ((), (), s32[]{:S(2)}) async-start(), calls=%async_computation.3 | async-start | bytes 229376 | tf_op jit(solution)/shard_map/psum | solution.py:200
  283.0 61.0 %copy-start.5 = (f32[32,8,512]{2,0,1:T(8,128)S(1)}, f32[32,8,512]{2,0,1:T(8,128)}, u32[]{:S(2)}) copy-start(f32[32,8,512]{2,0,1:T(8,128)} %get-tuple-element.367) | copy-start | bytes 1572868
  357.8 270.3 %all-reduce.38.cloned.1.call-start = ((), (), s32[]{:S(2)}) async-start(), calls=%async_computation.4 | async-start | bytes 229376 | tf_op jit(solution)/shard_map/psum | solution.py:199
  462.6 167.1 %copy-start.1 = (bf16[32,864]{1,0:T(8,128)(2,1)S(1)}, bf16[32,864]{1,0:T(8,128)(2,1)}, u32[]{:S(2)}) copy-start(bf16[32,864]{1,0:T(8,128)(2,1)} %param.16) | copy-start | bytes 165892
Sparse Core Ops, SparseCore 0:
  357.9 104.6 all-reduce.35
  465.0 72.2 all-reduce.37
